TPU v7x, 512 devices: a whole 4x8x8 slice. The times are simulated.
512 devices in a mesh: seq: 128 (over y, z, core), tp: 4 (over x).
Axes of the slice: x: 4, y: 8, z: 8, core: 2. Of those that a mesh axis runs over, the one named last changes fastest.
Arguments:
- features: bfloat16 [16384, 3, 4096], P('seq', None, 'tp'), may hold values from -6 to 6
- short_taps: bfloat16 [3, 3, 4096], P(None, None, 'tp'), may hold values from -3.5 to 3.5
- rates: float32 [4096, 16], P('tp'), may hold values from 6.1035156e-06 to 0.2
- residues: float32 [4096, 16], P('tp'), may hold values from -0.0625 to 0.0625
- skip: float32 [4096], P('tp'), may hold values from -6 to 6
- out_weight: bfloat16 [4096, 4096], P('seq', 'tp'), may hold values from -0.09375 to 0.09375
Outputs:
- layer_out: bfloat16 [16384, 4096], P('seq', 'tp')
All inputs are finite; a program needn't handle non-finite values.
Results may differ from a plain program's by a relative error of at most 0.025.
Values may be sent and summed in bfloat16 or wider, within the bound.
A program may use at most 128 MiB of HBM per device.

v0:
```python
import jax
import jax.numpy as jnp
from jax import lax
from jax.sharding import PartitionSpec as P

HIGH = lax.Precision.HIGHEST


def from_behind(x, axis, by):
    length = lax.axis_size(axis)
    pairs = [(i, i + by) for i in range(length) if 0 <= i + by < length]
    return lax.ppermute(x, axis, pairs)


def prefix(x, axis, join, neutral):
    place = lax.axis_index(axis)
    gathered = jax.tree.map(
        lambda a, kind: lax.all_gather(a.astype(kind), axis), x, (jnp.bfloat16, jnp.bfloat16)
    )
    state = jax.tree.map(lambda a, e: jnp.zeros_like(a) + jnp.asarray(e, a.dtype), x, neutral)

    def one(lap, state):
        return join(
            state,
            jax.tree.map(
                lambda a, own: lax.dynamic_index_in_dim(a, lap, 0, False).astype(own.dtype),
                gathered,
                x,
            ),
        )

    return lax.fori_loop(0, place, one, state)


def per_device(features, short_taps, rates, residues, skip, out_weight):
    tok_rows = features.shape[0]
    channels = features.shape[2]
    tap_count = short_taps.shape[1]
    last_rows = features[tok_rows - (tap_count - 1) :]
    before = from_behind(last_rows, "seq", 1)
    padded = jnp.concatenate([before, features], axis=0).astype(jnp.float32)
    tap_values = short_taps.astype(jnp.float32)
    mixed = tap_values[:, 0, :] * padded[tap_count - 1 :]
    for shift_rows in range(1, tap_count):
        lower = tap_count - 1 - shift_rows
        mixed = mixed + tap_values[:, shift_rows, :] * padded[lower : lower + tok_rows]
    signal = mixed[:, 1, :] * mixed[:, 2, :]
    piece_len = min(32, tok_rows)
    piece_count = tok_rows // piece_len
    rate_rows = rates.T
    residue_rows = residues.T
    offsets = jnp.arange(piece_len).astype(jnp.float32)
    short_filter = jnp.sum(
        residue_rows[None] * jnp.exp(-rate_rows[None] * offsets[:, None, None]), axis=1
    )
    positions = jnp.arange(piece_len)
    onehot = (
        positions[:, None, None] == positions[None, :, None] - positions[None, None, :]
    ).astype(jnp.float32)
    toeplitz = jnp.einsum("lc,lts->tsc", short_filter, onehot, precision=HIGH)
    blocks = signal.reshape(piece_count, piece_len, channels)
    near_part = jnp.einsum("tsc,msc->mtc", toeplitz, blocks, precision=HIGH)
    end_weight = jnp.exp(-rate_rows[None] * (piece_len - 1 - offsets)[:, None, None])
    block_ends = jnp.einsum("src,msc->mrc", end_weight, blocks, precision=HIGH)
    piece_index = jnp.arange(piece_count).astype(jnp.float32)
    piece_decay = jnp.exp(-rate_rows * piece_len)

    def enter_step(state, block_end):
        return (piece_decay * state + block_end, state)

    local_end, local_enter = lax.scan(enter_step, jnp.zeros_like(piece_decay), block_ends)

    def combine(earlier, following):
        return (
            earlier[0] + following[0],
            jnp.exp(-rate_rows * following[0]) * earlier[1] + following[1],
        )

    span_rows = jnp.full((1, 1), float(tok_rows), jnp.float32)
    identity = (jnp.zeros((1, 1), jnp.float32), jnp.zeros_like(local_end))
    _, entering = prefix((span_rows, local_end), "seq", combine, identity)
    incoming = (
        local_enter
        + jnp.exp(-rate_rows[None] * piece_len * piece_index[:, None, None]) * entering[None]
    )
    gain_weight = residue_rows[None] * jnp.exp(-rate_rows[None] * (offsets + 1.0)[:, None, None])
    far_part = jnp.einsum("trc,mrc->mtc", gain_weight, incoming, precision=HIGH)
    conv = (near_part + far_part).reshape(tok_rows, channels) + skip[None] * signal
    gated = (mixed[:, 0, :] * conv).astype(jnp.bfloat16)
    partial_value = lax.dot_general(
        gated,
        lax.all_gather(out_weight, "seq", axis=0, tiled=True),
        (((1,), (1,)), ((), ())),
        preferred_element_type=jnp.float32,
    )
    result = lax.psum_scatter(
        partial_value.astype(jnp.bfloat16), "tp", scatter_dimension=1, tiled=True
    )
    return result


def solution(mesh):
    in_specs = (
        P("seq", None, "tp"),
        P(None, None, "tp"),
        P("tp", None),
        P("tp", None),
        P("tp"),
        P("seq", "tp"),
    )
    out_specs = P("seq", "tp")
    return jax.shard_map(
        per_device, mesh=mesh, in_specs=in_specs, out_specs=out_specs, check_vma=False
    )
```

profile of v0, /device:TPU:1, one launch (start us, length us, event | category | flops | bytes accessed | tf_op | source)
XLA Modules:
  0.0 672.4 jit_solution(6074333785399840641)
XLA Ops:
  6.5 0.8 slice.31
  7.4 5.4 collective-permute-start
  12.7 0.8 negate_bitcast_fusion
  13.6 0.9 broadcast_multiply_fusion
  14.4 0.9 fusion.26
  16.1 1.4 maximum_convert_fusion
  18.1 1.1 copy-done
  19.1 0.8 copy.24
  20.0 14.9 %fusion.12 = f32[4,16,1024]{1,0,2:T(4,128)} fusion(f32[4,32,1024]{1,0,2:T(4,128)S(1)} %copy.24, f32[32]{0:T(128)S(1)} %broadcast_subtract_fusion, f32[16,1024]{0,1:T(8,128)S(1)} %copy.22), kind=kOutput, calls=%fused_computation.19 | convolution fusion | flops 25690112 | bytes 852096 | tf_op jit(solution)/shard_map/src,msc->mrc/dot_general | solution.py:64
  34.9 1.9 copy.27
  36.7 2.7 while.28
  41.3 11.8 %multiply_reduce_fusion = f32[32,1024]{0,1:T(8,128)S(1)} fusion(f32[32]{0:T(128)S(1)} %iota_convert_fusion.1, f32[16,1024]{0,1:T(8,128)S(1)} %copy.22, f32[16,1024]{0,1:T(8,128)S(1)} %copy.21), kind=kLoop, calls=%fused_computation.11 | loop fusion | flops 1540096 | bytes 262272 | tf_op jit(solution)/shard_map/reduce_sum | solution.py:53
  53.1 3.8 fusion.22
  56.9 14.3 %copy.25 = f32[32,32,1024]{1,0,2:T(8,128)} copy(f32[32,32,1024]{2,1,0:T(8,128)} %fusion.22) | data formatting | bytes 8388608 | tf_op jit(solution)/shard_map/lc,lts->tsc/dot_general | solution.py:60
  71.2 1.3 dynamic-slice
  73.3 251.8 %all-reduce = bf16[128]{0:T(256)(128)(2,1)S(1)} all-reduce(bf16[128]{0:T(256)(128)(2,1)S(1)} %dynamic-update-slice), channel_id=1, replica_groups=mesh['seq'=128,'tp'=4] {'seq'}, use_global_device_ids=true, to_apply=%add | all-reduce | flops 128 | bytes 512
  325.1 29.4 %fusion.27 = f32[1024,4,32]{2,1,0:T(4,128)} fusion(f32[4,32,1024]{1,0,2:T(4,128)S(1)} %copy.24, f32[32,32,1024]{1,0,2:T(8,128)} %copy.25), kind=kOutput, calls=%fused_computation.49 | convolution fusion | flops 50331648 | bytes 5242880 | tf_op jit(solution)/shard_map/tsc,msc->mtc/dot_general | solution.py:62
  354.5 2.3 while.27
  356.8 1.8 multiply_add_fusion
  358.6 2.6 copy.28
  361.2 12.9 %add_bitcast_fusion = f32[4,32,1024]{1,0,2:T(4,128)} fusion(f32[1024,4,32]{2,1,0:T(4,128)S(1)} %copy-done.2, f32[4,16,1024]{1,0,2:T(4,128)} %copy.28, f32[32]{0:T(128)S(1)} %broadcast_add_fusion, f32[16,1024]{0,1:T(8,128)S(1)} %copy.22, f32[16,1024]{0,1:T(8,128)S(1)} %copy.21), kind=kOutput, calls=%fused_computation.18 | convolution fusion | flops 26345472 | bytes 1441920 | tf_op jit(solution)/shard_map/trc,mrc->mtc/dot_general | solution.py:87
  374.0 2.0 copy.29
  376.3 7.2 %convolution_convert_fusion = bf16[128,4096]{1,0:T(8,128)(2,1)} fusion(bf16[128,1024]{1,0:T(8,128)(2,1)S(1)} %fusion.20, bf16[4096,1024]{1,0:T(8,128)(2,1)} %all-gather.4.cloned.1.call-done), kind=kOutput, calls=%fused_computation.12 | convolution fusion | flops 1074266112 | bytes 9699328 | tf_op jit(solution)/shard_map/dot_general | solution.py:90
  383.5 282.3 %reduce-scatter.2.cloned.1.call-done = bf16[128,1024]{1,0:T(8,128)(2,1)} async-done(((bf16[128,4096]{1,0:T(8,128)(2,1)}), bf16[128,1024]{1,0:T(8,128)(2,1)}) %reduce-scatter.2.cloned.1.call-update) | async-done | bytes 262160 | tf_op jit(solution)/shard_map/reduce_scatter | solution.py:96
  (46 shorter events, 8.2 us)
Async XLA Ops:
  6.5 347.9 %all-gather.6.cloned.1.call-start = ((), (), s32[]{:S(2)}) async-start(), calls=%async_computation.3 | async-start | bytes 4227072 | tf_op jit(solution)/shard_map/all_gather | solution.py:18
  7.4 8.8 %collective-permute-start = (bf16[2,3,1024]{2,0,1:T(2,128)(2,1)S(1)}, bf16[2,3,1024]{2,0,1:T(2,128)(2,1)S(1)}, u32[]{:S(2)}, u32[]{:S(2)}) collective-permute-start(bf16[2,3,1024]{2,0,1:T(2,128)(2,1)S(1)} %slice.31), channel_id=1, source_target_pairs={{0,4},{4,8},{8,12},{12,16},{16,20},{20,24},{24,28},{28,32},{32,36}... | collective-permute-start | bytes 36872 | tf_op jit(solution)/shard_map/ppermute | solution.py:12
  18.0 1.1 copy-start
  34.9 6.2 copy-start.3
  40.1 336.2 %all-gather.4.cloned.1.call-start = ((), (), s32[]{:S(2)}) async-start(), calls=%async_computation.1 | async-start | bytes 8454144 | tf_op jit(solution)/shard_map/all_gather | solution.py:92
  40.8 625.0 %reduce-scatter.2.cloned.1.call-start = ((), (), s32[]{:S(2)}) async-start(), calls=%async_computation.2 | async-start | bytes 1310720 | tf_op jit(solution)/shard_map/reduce_scatter | solution.py:96
  354.5 6.7 copy-start.2
  374.0 2.0 copy-start.1
  374.0 2.0 copy-start.4
Sparse Core Ops, SparseCore 0:
  40.2 87.7 all-gather.5
  131.1 84.4 all-gather.3
  383.7 282.1 reduce-scatter.1
where the time goes:
time: 683 us; the launch traced here: 672 us
  waiting for transfers between devices  284 us (42%)
  blocking collectives  252 us (37%)
  matrix products  68.1 us (10%)
  local copies, waits for them, and re-layouts  27.6 us (4%)
  other arithmetic  21.4 us (3%)
  between operations  13.3 us (2%)
    reduce_scatter x1, waiting for transfers between devices, per_device(): lax.psum_scatter(partial_value.astype(jnp.bfloat16), 'tp', scatter_dimens...  282 us
    unnamed x1, blocking collectives  252 us
    dot_general x1, matrix products, per_device(): near_part = jnp.einsum('tsc,msc->mtc', toeplitz, blocks, precision=HIGH)  29.4 us
    dot_general x1, matrix products, per_device(): block_ends = jnp.einsum('src,msc->mrc', end_weight, blocks, precision=HIGH)  14.9 us
    dot_general x1, local copies, waits for them, and re-layouts, per_device(): toeplitz = jnp.einsum('lc,lts->tsc', short_filter, onehot, precision=HIGH)  14.3 us
  transfers between devices with their start and end apart: 4, of which 2 were waited for; matrix products, arithmetic and copies ran while one was open for 13% of the time, Pallas kernels for 0%

commit v1 on v0

v1 whole, which is shorter than its diff:
```python
import jax
import jax.numpy as jnp
from jax import lax
from jax.experimental import pallas as pl
from jax.experimental.pallas import tpu as pltpu
from jax.sharding import PartitionSpec as P

MESH = pl.DeviceIdType.MESH
F32, BF16 = jnp.float32, jnp.bfloat16
N = 8
TOK, CH, POLES, OUTS = 128, 1024, 16, 4096
BLK, STEPS = 8, 16
LANES = CH // 128
HALF = CH // 2
DIRS = (1, -1)


class Copies:
    def __init__(self, send_sem, recv_sem):
        self.send_sem, self.recv_sem, self.used, self.sent = send_sem, recv_sem, 0, []

    def ids(self, count):
        first = self.used
        self.used += count
        return first

    def make(self, index, src, dst, device):
        return pltpu.make_async_remote_copy(
            src_ref=src,
            dst_ref=dst,
            send_sem=self.send_sem.at[index],
            recv_sem=self.recv_sem.at[index],
            device_id=device,
            device_id_type=MESH,
        )

    def send(self, index, src, dst, device):
        copy = self.make(index, src, dst, device)
        copy.start()
        self.sent.append(copy)


def kernel(
    feat_hbm, taps_ref, rate_ref, res_ref, skip_ref, w_hbm, out_ref,
    wbuf, featb, halo, x, u, m0, taps, dec, ent, ends, ends_b, sib_ends,
    chip_end, y_in, col_b, colp_b, z_in, col, enter, enter_b, sib_enter,
    g, gb, own, part, diag, arrived, send_sem, recv_sem, local_sem,
):
    s, t = lax.axis_index("seq"), lax.axis_index("tp")
    c, q = lax.rem(s, 2), lax.div(s, 2)
    z, y = lax.rem(q, N), lax.div(q, N)
    copies = Copies(send_sem, recv_sem)

    def at(y_of, z_of, c_of):
        return ((y_of * N + z_of) * 2 + c_of, t)

    def ring(i, by):
        return lax.rem(i + by + N, N)

    sib = at(y, z, 1 - c)
    after, before = lax.rem(s + 1, 2 * N * N), lax.rem(s + 2 * N * N - 1, 2 * N * N)
    x_next, x_prev, x_far = lax.rem(t + 1, 4), lax.rem(t + 3, 4), lax.rem(t + 2, 4)

    load_w = [
        pltpu.make_async_copy(w_hbm.at[pl.ds(16 * p, 16)], wbuf.at[y, z, c, p], local_sem.at[p])
        for p in range(2)
    ]
    load_f = pltpu.make_async_copy(feat_hbm, featb, local_sem.at[2])
    for copy in load_w:
        copy.start()
    load_f.start()
    barrier = pltpu.get_barrier_semaphore()
    far_seq = jnp.where(c == 0, before, after)
    partners = [sib, (far_seq, t), (s, x_next), (s, x_prev)]
    for by in DIRS:
        partners += [at(y, ring(z, by), c), at(ring(y, by), z, c)]
    for partner in partners:
        pl.semaphore_signal(barrier, inc=1, device_id=partner, device_id_type=MESH)
    pl.semaphore_wait(barrier, len(partners))

    streams = [(p, d) for d in (0, 1) for p in (0, 1)]
    ring1 = {st: copies.ids(4) for st in streams}
    ring2 = {st: copies.ids(8) for st in streams}
    fwd2 = {st: copies.ids(8) for st in streams}
    fwd1 = {p: copies.ids(1) for p in (0, 1)}

    def lanes(half):
        return pl.ds(0, CH) if half is None else pl.ds(half * HALF, HALF)

    def target(p, d, first):
        along_z = (p == 0) == first
        return at(y, ring(z, DIRS[d]), c) if along_z else at(ring(y, DIRS[d]), z, c)

    def piece1(p, origin, half):
        if p == 0:
            return wbuf.at[y, origin, c, 0, :, lanes(half)]
        return wbuf.at[origin, z, c, 1, :, lanes(half)]

    def piece2(p, origin, half, core):
        if p == 0:
            return wbuf.at[origin, :, core, 0, :, lanes(half)]
        return wbuf.at[:, origin, core, 1, :, lanes(half)]

    def home(p, first):
        return z if (p == 0) == first else y

    def send1(st, k):
        p, d = st
        ref = piece1(p, ring(home(p, True), -DIRS[d] * k), d if k == 3 else None)
        copies.send(ring1[st] + k, ref, ref, target(p, d, True))

    def recv1(st, k):
        p, d = st
        ref = piece1(p, ring(home(p, True), -DIRS[d] * (k + 1)), d if k == 3 else None)
        copies.make(ring1[st] + k, ref, ref, sib).wait_recv()

    def send2(st, k, h):
        p, d = st
        ref = piece2(p, ring(home(p, False), -DIRS[d] * k), h, c)
        copies.send(ring2[st] + 2 * k + h, ref, ref, target(p, d, False))

    def recv2(st, k, h):
        p, d = st
        ref = piece2(p, ring(home(p, False), -DIRS[d] * (k + 1)), h, c)
        copies.make(ring2[st] + 2 * k + h, ref, ref, sib).wait_recv()

    def forward2(st, k, h):
        p, d = st
        ref = piece2(p, ring(home(p, False), -DIRS[d] * (k + 1)), h, c)
        copies.send(fwd2[st] + 2 * k + h, ref, ref, sib)

    def forwarded2(st, k, h):
        p, d = st
        ref = piece2(p, ring(home(p, False), -DIRS[d] * (k + 1)), h, 1 - c)
        copies.make(fwd2[st] + 2 * k + h, ref, ref, sib).wait_recv()

    def phase1(k):
        for st in streams:
            recv1(st, k)
            if k < 3:
                send1(st, k + 1)

    def phase2(k, h):
        for st in streams:
            if k == 3 and h != st[1]:
                continue
            recv2(st, k, h)
            if k < 2 or (k == 2 and h == st[1]):
                send2(st, k + 1, h)
            forward2(st, k, h)

    for copy in load_w:
        copy.wait()
    for st in streams:
        send1(st, 0)
    halo_id = copies.ids(1)
    copies.send(halo_id, feat_hbm.at[:, pl.ds(TOK - 8, 8), :], halo, (after, t))

    taps[...] = taps_ref[...].astype(F32)
    rate = rate_ref[...]
    for k, span in enumerate((1, 16, 32, 64, 128)):
        dec[k] = jnp.exp(-rate * float(span))
    load_f.wait()
    for group in range(3):
        for lane in range(LANES):
            cut = slice(lane * 128, (lane + 1) * 128)
            x[group, lane, pl.ds(8, TOK), :] = featb[group, :, cut].astype(F32)
    phase1(0)
    copies.make(halo_id, halo, halo, sib).wait_recv()
    for group in range(3):
        for lane in range(LANES):
            cut = slice(lane * 128, (lane + 1) * 128)
            edge = jnp.where(s > 0, halo[group, :, cut].astype(F32), 0.0)
            x[group, lane, pl.ds(0, 8), :] = edge

    def row(ref, *index):
        return jnp.broadcast_to(ref[index], (BLK, 128))

    def mix(lane, carry):
        col_at = pl.ds(pl.multiple_of(lane * 128, 128), 128)

        def mixed(group):
            w = [row(taps, group, pl.ds(k, 1), col_at) for k in range(3)]
            v = [x[group, lane, pl.ds(6 + i, BLK, stride=STEPS), :] for i in range(STEPS + 2)]
            return [w[0] * v[i + 2] + w[1] * v[i + 1] + w[2] * v[i] for i in range(STEPS)]

        one, two = mixed(1), mixed(2)
        for i in range(STEPS):
            u[i, :, col_at] = one[i] * two[i]
        for i, value in enumerate(mixed(0)):
            m0[i, :, col_at] = value
        return carry

    lax.fori_loop(0, LANES, mix, 0)
    phase1(1)

    block = lax.broadcasted_iota(jnp.int32, (BLK, 128), 0)

    def shifted(value, by):
        return jnp.where(block >= by, pltpu.roll(value, by, axis=0), 0.0)

    def pass1(lane, carry):
        col_at = pl.ds(pl.multiple_of(lane * 128, 128), 128)
        values = [u[i, :, col_at] for i in range(STEPS)]
        for pole in range(POLES):
            step = row(dec, 0, pl.ds(pole, 1), col_at)
            state = values[0]
            for i in range(1, STEPS):
                state = step * state + values[i]
            for k, by in ((1, 1), (2, 2), (3, 4)):
                state = state + row(dec, k, pl.ds(pole, 1), col_at) * shifted(state, by)
            ent[pole, :, col_at] = shifted(state, 1)
            ends[pl.ds(pole, 1), col_at] = state[BLK - 1 :, :]
        return carry

    lax.fori_loop(0, LANES, pass1, 0)
    ends_b[...] = ends[...].astype(BF16)
    sib_id = copies.ids(1)
    copies.send(sib_id, ends_b, sib_ends, sib)
    phase1(2)

    mine = pl.ds(pl.multiple_of(c * HALF, HALF), HALF)
    rate_h = rate_ref[:, mine]

    def decay(tokens):
        return jnp.exp(-rate_h * float(tokens))

    copies.make(sib_id, sib_ends, sib_ends, sib).wait_recv()
    own_end, other_end = ends[:, mine], sib_ends[:, mine].astype(F32)
    first_end = jnp.where(c == 0, own_end, other_end)
    second_end = jnp.where(c == 0, other_end, own_end)
    total = decay(128) * first_end + second_end
    chip_end[...] = total.astype(BF16)
    phase1(3)

    y_id, z_id, zw_id = copies.ids(N), copies.ids(N), copies.ids(1)
    for k in range(1, N):

        @pl.when(y + k < N)
        def _(k=k):
            copies.make(y_id + k, chip_end, y_in.at[k], at(y + k, z, c)).start()

    for h in (0, 1):
        for st in streams:
            send2(st, 0, h)
    for p in (0, 1):
        ref = piece2(p, home(p, False), None, c)
        copies.send(fwd1[p], ref, ref, sib)

    col[...] = jnp.zeros_like(col)
    for k in range(1, N):

        @pl.when(y >= k)
        def _(k=k):
            copies.make(y_id + k, y_in.at[k], y_in.at[k], sib).wait_recv()
            col[...] += decay(2048 * (k - 1)) * y_in[k].astype(F32)

    col_b[...] = col[...].astype(BF16)
    colp_b[...] = (total + decay(2048) * col[...]).astype(BF16)
    for k in range(1, N):

        @pl.when(z + k < N)
        def _(k=k):
            copies.make(z_id + k, colp_b, z_in.at[k], at(y, z + k, c)).start()

        @pl.when(z + k >= N)
        def _(k=k):
            copies.make(z_id + k, col_b, z_in.at[k], at(y, z + k - N, c)).start()

    phase2(0, 0)
    phase2(0, 1)

    state = decay(256 * 7) * col[...]
    for k in range(1, N):
        copies.make(z_id + k, z_in.at[k], z_in.at[k], sib).wait_recv()
        state = state + decay(256 * (k - 1)) * z_in[k].astype(F32)
    enter_b[...] = state.astype(BF16)
    enter[:, mine] = state
    enter_id = copies.ids(1)
    copies.send(enter_id, enter_b, sib_enter, sib)
    phase2(1, 0)
    copies.make(enter_id, sib_enter, sib_enter, sib).wait_recv()
    theirs = pl.ds(pl.multiple_of((1 - c) * HALF, HALF), HALF)
    enter[:, theirs] = sib_enter[...].astype(F32)

    @pl.when(c == 1)
    def _():
        enter[...] = dec[4] * enter[...] + sib_ends[...].astype(F32)

    phase2(1, 1)

    far = (-float(STEPS)) * block.astype(F32)

    def pass2(lane, carry):
        col_at = pl.ds(pl.multiple_of(lane * 128, 128), 128)
        values = [u[i, :, col_at] for i in range(STEPS)]
        skip = row(skip_ref, pl.ds(0, 1), col_at)

        def one_pole(pole, sums):
            step = row(dec, 0, pl.ds(pole, 1), col_at)
            gain = row(res_ref, pl.ds(pole, 1), col_at)
            reach = jnp.exp(far * row(rate_ref, pl.ds(pole, 1), col_at))
            state = ent[pole, :, col_at] + reach * row(enter, pl.ds(pole, 1), col_at)
            out = []
            for i in range(STEPS):
                state = step * state + values[i]
                out.append(sums[i] + gain * state)
            return out

        sums = [skip * value for value in values]
        for pole in range(POLES):
            sums = one_pole(pole, sums)
        for i in range(STEPS):
            g[lane, pl.ds(i, BLK, stride=STEPS), :] = m0[i, :, col_at] * sums[i]
        return carry

    lax.fori_loop(0, LANES, pass2, 0)
    for lane in range(LANES):
        gb[:, lane * 128 : (lane + 1) * 128] = g[lane].astype(BF16)

    phase2(2, 0)
    phase2(2, 1)
    phase2(3, 0)
    phase2(3, 1)
    for p in (0, 1):
        ref = piece2(p, home(p, False), None, 1 - c)
        copies.make(fwd1[p], ref, ref, sib).wait_recv()
    for k in range(4):
        for h in (0, 1):
            for st in streams:
                if k < 3 or h == st[1]:
                    forwarded2(st, k, h)

    def project(j, n):
        w = wbuf[2 * j + n // 2, pl.ds(4 * (n % 2), 4)].reshape(256, CH)
        return lax.dot_general(
            gb[...], w, (((1,), (1,)), ((), ())), preferred_element_type=F32
        )

    def chunk(slot, j):
        for n in range(4):
            part[slot, :, n * 256 : (n + 1) * 256] = project(j, n).astype(BF16)

    top, low = pl.ds(0, TOK // 2), pl.ds(TOK // 2, TOK // 2)
    rs = copies.ids(6)
    next_dev, prev_dev = (s, x_next), (s, x_prev)
    chunk(0, x_far)
    copies.send(rs, part.at[0, top], diag.at[0], prev_dev)
    copies.send(rs + 1, part.at[0, low], diag.at[1], next_dev)
    chunk(1, x_next)
    copies.send(rs + 2, part.at[1, top], arrived.at[0, top], next_dev)
    chunk(2, x_prev)
    copies.send(rs + 3, part.at[2, low], arrived.at[1, low], prev_dev)
    copies.make(rs + 1, diag.at[1], diag.at[1], sib).wait_recv()
    part[1, low, :] = (part[1, low, :].astype(F32) + diag[1].astype(F32)).astype(BF16)
    copies.send(rs + 4, part.at[1, low], arrived.at[0, low], next_dev)
    copies.make(rs, diag.at[0], diag.at[0], sib).wait_recv()
    part[2, top, :] = (part[2, top, :].astype(F32) + diag[0].astype(F32)).astype(BF16)
    copies.send(rs + 5, part.at[2, top], arrived.at[1, top], prev_dev)
    for n in range(4):
        own[:, n * 256 : (n + 1) * 256] = project(t, n)
    copies.make(rs + 2, arrived.at[0, top], arrived.at[0, top], sib).wait_recv()
    copies.make(rs + 3, arrived.at[1, low], arrived.at[1, low], sib).wait_recv()
    copies.make(rs + 4, arrived.at[0, low], arrived.at[0, low], sib).wait_recv()
    copies.make(rs + 5, arrived.at[1, top], arrived.at[1, top], sib).wait_recv()
    out_ref[...] = (own[...] + arrived[0].astype(F32) + arrived[1].astype(F32)).astype(BF16)

    for copy in copies.sent:
        copy.wait_send()
    for k in range(1, N):

        @pl.when(y + k < N)
        def _(k=k):
            copies.make(y_id + k, chip_end, y_in.at[k], sib).wait_send()

        copies.make(z_id + k, col_b, z_in.at[k], sib).wait_send()


N_COPIES = 120


def per_device(features, short_taps, rates, residues, skip, out_weight):
    vmem, hbm = pl.BlockSpec(memory_space=pltpu.VMEM), pl.BlockSpec(memory_space=pl.ANY)
    return pl.pallas_call(
        kernel,
        out_shape=jax.ShapeDtypeStruct((TOK, CH), BF16),
        in_specs=[hbm, vmem, vmem, vmem, vmem, hbm],
        out_specs=vmem,
        scratch_shapes=[
            pltpu.VMEM((N, N, 2, 2, 16, CH), BF16),
            pltpu.VMEM((3, TOK, CH), BF16),
            pltpu.VMEM((3, 8, CH), BF16),
            pltpu.VMEM((3, LANES, TOK + 8, 128), F32),
            pltpu.VMEM((STEPS, BLK, CH), F32),
            pltpu.VMEM((STEPS, BLK, CH), F32),
            pltpu.VMEM((3, 3, CH), F32),
            pltpu.VMEM((5, POLES, CH), F32),
            pltpu.VMEM((POLES, BLK, CH), F32),
            pltpu.VMEM((POLES, CH), F32),
            pltpu.VMEM((POLES, CH), BF16),
            pltpu.VMEM((POLES, CH), BF16),
            pltpu.VMEM((POLES, HALF), BF16),
            pltpu.VMEM((N, POLES, HALF), BF16),
            pltpu.VMEM((POLES, HALF), BF16),
            pltpu.VMEM((POLES, HALF), BF16),
            pltpu.VMEM((N, POLES, HALF), BF16),
            pltpu.VMEM((POLES, HALF), F32),
            pltpu.VMEM((POLES, CH), F32),
            pltpu.VMEM((POLES, HALF), BF16),
            pltpu.VMEM((POLES, HALF), BF16),
            pltpu.VMEM((LANES, TOK, 128), F32),
            pltpu.VMEM((TOK, CH), BF16),
            pltpu.VMEM((TOK, CH), F32),
            pltpu.VMEM((3, TOK, CH), BF16),
            pltpu.VMEM((2, TOK // 2, CH), BF16),
            pltpu.VMEM((2, TOK, CH), BF16),
            pltpu.SemaphoreType.DMA((N_COPIES,)),
            pltpu.SemaphoreType.DMA((N_COPIES,)),
            pltpu.SemaphoreType.DMA((3,)),
        ],
        compiler_params=pltpu.CompilerParams(
            collective_id=0, has_side_effects=True, vmem_limit_bytes=48 << 20
        ),
        name="hyena",
    )(
        features.transpose(1, 0, 2),
        short_taps,
        rates.T,
        residues.T,
        skip.reshape(1, CH),
        out_weight,
    )


def solution(mesh):
    in_specs = (
        P("seq", None, "tp"),
        P(None, None, "tp"),
        P("tp", None),
        P("tp", None),
        P("tp"),
        P("seq", "tp"),
    )
    out_specs = P("seq", "tp")
    return jax.shard_map(
        per_device, mesh=mesh, in_specs=in_specs, out_specs=out_specs, check_vma=False
    )
```

time: 683 us -> 73.5 us (0.11); the launches traced: 672 us -> 73.1 us
  waiting for transfers between devices: 284 us -> 0 us
  blocking collectives: 252 us -> 0 us
  matrix products: 68.1 us -> 0 us
  Pallas kernels: 0 us -> 67.3 us
  local copies, waits for them, and re-layouts: 27.6 us -> 5.78 us
  other arithmetic: 21.4 us -> 0 us
  between operations: 13.3 us -> 0.02 us
    reduce_scatter x1 -> x0, waiting for transfers between devices: 282 us -> none  [per_device(): lax.psum_scatter(partial_value.astype(jnp.bfloat16), 'tp', scatter_dimens...]
    unnamed x1 -> x0, blocking collectives: 252 us -> none
    dot_general x5 -> x0, matrix products: 68.1 us -> none  [the longest x1 29.4 us: per_device(): near_part = jnp.einsum('tsc,msc->mtc', toeplitz, blocks, precision=HIGH)]
    pallas_call x0 -> x1, Pallas kernels: none -> 67.3 us  [per_device(): pl.pallas_call(kernel, out_shape=jax.ShapeDtypeStruct((TOK, CH), BF16), i...]
    dot_general x1 -> x0, local copies, waits for them, and re-layouts: 14.3 us -> none  [per_device(): toeplitz = jnp.einsum('lc,lts->tsc', short_filter, onehot, precision=HIGH)]
    reduce_sum x1 -> x0, other arithmetic: 11.8 us -> none  [per_device(): jnp.sum(residue_rows[None] * jnp.exp(-rate_rows[None] * offsets[:, None,...]
  transfers between devices with their start and end apart: 4 -> 0, of which waited for: 2 -> 0; matrix products, arithmetic and copies ran while one was open for 13% -> 0% of each run, Pallas kernels for 0% -> 0%
where the time goes in v1:
time: 73.5 us; the launch traced here: 73.1 us
  Pallas kernels  67.3 us (92%)
  local copies, waits for them, and re-layouts  5.78 us (8%)
    pallas_call x1, Pallas kernels, per_device(): pl.pallas_call(kernel, out_shape=jax.ShapeDtypeStruct((TOK, CH), BF16), i...  67.3 us
    unnamed x13, local copies, waits for them, and re-layouts  5.78 us

profile of v1, /device:TPU:1, one launch (start us, length us, event | category | flops | bytes accessed | tf_op | source)
XLA Modules:
  0.0 73.1 jit_solution(14987805078570461607)
XLA Ops:
  0.0 0.0 copy-start.5
  0.0 0.7 copy-done.5
  0.7 0.0 copy-start
  0.7 1.1 %copy-done = bf16[128,3,1024]{2,0,1:T(8,128)(2,1)S(1)} copy-done((bf16[128,3,1024]{2,0,1:T(8,128)(2,1)S(1)}, bf16[128,3,1024]{2,0,1:T(8,128)(2,1)}, u32[]{:S(2)}) %copy-start) | copy-done | bytes 786456
  1.8 0.0 copy-start.1
  1.8 0.8 %copy-done.1 = f32[1024,16]{0,1:T(8,128)S(1)} copy-done((f32[1024,16]{0,1:T(8,128)S(1)}, f32[1024,16]{0,1:T(8,128)}, u32[]{:S(2)}) %copy-start.1) | copy-done | bytes 65560
  2.7 0.0 copy-start.2
  2.7 0.8 %copy-done.2 = f32[1024,16]{0,1:T(8,128)S(1)} copy-done((f32[1024,16]{0,1:T(8,128)S(1)}, f32[1024,16]{0,1:T(8,128)}, u32[]{:S(2)}) %copy-start.2) | copy-done | bytes 65560
  3.5 0.0 copy-start.3
  3.5 0.8 %copy-done.3 = bf16[32,1024]{1,0:T(8,128)(2,1)S(1)} copy-done((bf16[32,1024]{1,0:T(8,128)(2,1)S(1)}, bf16[32,1024]{1,0:T(8,128)(2,1)}, u32[]{:S(2)}) %copy-start.3) | copy-done | bytes 65560
  4.3 0.0 copy-start.4
  4.3 0.7 %copy-done.4 = bf16[3,3,1024]{2,1,0:T(4,128)(2,1)S(1)} copy-done((bf16[3,3,1024]{2,1,0:T(4,128)(2,1)S(1)}, bf16[3,3,1024]{2,1,0:T(4,128)(2,1)}, u32[]{:S(2)}) %copy-start.4) | copy-done | bytes 18456
  5.1 67.3 %hyena.1 = bf16[128,1024]{1,0:T(8,128)(2,1)S(1)} custom-call(bf16[3,128,1024]{2,1,0:T(8,128)(2,1)S(1)} %bitcast.4, bf16[3,3,1024]{2,1,0:T(4,128)(2,1)S(1)} %copy-done.4, f32[16,1024]{1,0:T(8,128)S(1)} %bitcast.5, f32[16,1024]{1,0:T(8,128)S(1)} %bitcast.6, f32[1,1024]{1,0:T(1,128)S(1)} %bitcast.7, bf16[32,1024]{1,0:T(8,128)(2,1)S(1)} %copy-done.3), custom_call_target="tpu_custom_call" | custom-call | tf_op jit(solution)/shard_map/hyena/pallas_call | solution.py:384
  72.4 0.7 copy.8
Async XLA Ops:
  0.0 0.7 copy-start.5
  0.7 1.1 %copy-start = (bf16[128,3,1024]{2,0,1:T(8,128)(2,1)S(1)}, bf16[128,3,1024]{2,0,1:T(8,128)(2,1)}, u32[]{:S(2)}) copy-start(bf16[128,3,1024]{2,0,1:T(8,128)(2,1)} %param.6) | copy-start | bytes 2359300
  1.8 0.8 %copy-start.1 = (f32[1024,16]{0,1:T(8,128)S(1)}, f32[1024,16]{0,1:T(8,128)}, u32[]{:S(2)}) copy-start(f32[1024,16]{0,1:T(8,128)} %param.8) | copy-start | bytes 196612
  2.7 0.8 %copy-start.2 = (f32[1024,16]{0,1:T(8,128)S(1)}, f32[1024,16]{0,1:T(8,128)}, u32[]{:S(2)}) copy-start(f32[1024,16]{0,1:T(8,128)} %param.9) | copy-start | bytes 196612
  3.5 0.8 %copy-start.3 = (bf16[32,1024]{1,0:T(8,128)(2,1)S(1)}, bf16[32,1024]{1,0:T(8,128)(2,1)}, u32[]{:S(2)}) copy-start(bf16[32,1024]{1,0:T(8,128)(2,1)} %w_hbm.1) | copy-start | bytes 196612
  4.3 0.7 %copy-start.4 = (bf16[3,3,1024]{2,1,0:T(4,128)(2,1)S(1)}, bf16[3,3,1024]{2,1,0:T(4,128)(2,1)}, u32[]{:S(2)}) copy-start(bf16[3,3,1024]{2,1,0:T(4,128)(2,1)} %taps_ref.1) | copy-start | bytes 55300

commit v2 on v1

v2 whole, which is shorter than its diff:
```python
import functools

import jax
import jax.numpy as jnp
from jax import lax
from jax.experimental import pallas as pl
from jax.experimental.pallas import tpu as pltpu
from jax.sharding import PartitionSpec as P

MESH = pl.DeviceIdType.MESH
F32, BF16 = jnp.float32, jnp.bfloat16
N = 8
TOK, CH, POLES, OUTS = 128, 1024, 16, 4096
BLK, STEPS = 8, 16
LANES = CH // 128
HALF = CH // 2
DIRS = (1, -1)
POOL = 64
GROUPS = ((0, 1), (1, 3), (3, 5), (5, 7), (7, 8))
OFFSETS = ((0,), (1, -1), (2, -2), (3, -3), (4,))
WIDE = 512


class Copies:
    def __init__(self, send_sem, recv_sem):
        self.send_sem, self.recv_sem, self.used, self.held = send_sem, recv_sem, 0, POOL
        self.pool, self.turn = {}, 0

    def ids(self, count):
        self.used += count
        return self.used - count

    def send_ids(self, count):
        self.held += count
        return self.held - count

    def make(self, index, src, dst, device, held=0):
        return pltpu.make_async_remote_copy(
            src_ref=src,
            dst_ref=dst,
            send_sem=self.send_sem.at[held],
            recv_sem=self.recv_sem.at[index],
            device_id=device,
            device_id_type=MESH,
        )

    def send(self, index, src, dst, device):
        held = self.turn % POOL
        self.turn += 1
        if held in self.pool:
            self.pool[held].wait_send()
        self.pool[held] = self.make(index, src, dst, device, held)
        self.pool[held].start()


def kernel(
    feat_hbm, taps_hbm, rate_hbm, res_hbm, skip_hbm, w_hbm, out_ref,
    wbuf, featb, halo, x, u, m0, taps_ref, rate_ref, res_ref, skip_ref, taps, dec,
    ent, ends, ends_b, sib_ends, chip_end, y_in, col_b, colp_b, z_in, col, enter,
    enter_b, sib_enter, g, gb, own, part, diag, arrived,
    send_sem, recv_sem, local_sem, here_sem,
):
    s, t = lax.axis_index("seq"), lax.axis_index("tp")
    c, q = lax.rem(s, 2), lax.div(s, 2)
    z, y = lax.rem(q, N), lax.div(q, N)
    copies = Copies(send_sem, recv_sem)

    def at(y_of, z_of, c_of):
        return ((y_of * N + z_of) * 2 + c_of, t)

    def ring(i, by):
        return lax.rem(i + by + N, N)

    sib = at(y, z, 1 - c)
    after, before = lax.rem(s + 1, 2 * N * N), lax.rem(s + 2 * N * N - 1, 2 * N * N)
    x_next, x_prev, x_far = lax.rem(t + 1, 4), lax.rem(t + 3, 4), lax.rem(t + 2, 4)

    loads = []

    def load(src, dst):
        copy = pltpu.make_async_copy(src, dst, local_sem.at[len(loads)])
        copy.start()
        loads.append(copy)

    barrier = pltpu.get_barrier_semaphore()
    far_seq = jnp.where(c == 0, before, after)
    around = [(y_z, by) for y_z in (0, 1) for by in DIRS]
    around = [at(ring(y, by), z, c) if y_z else at(y, ring(z, by), c) for y_z, by in around]
    partners = [sib, (far_seq, t), (s, x_next), (s, x_prev)] + around
    for partner in partners:
        pl.semaphore_signal(barrier, inc=1, device_id=partner, device_id_type=MESH)
    for p in range(2):
        load(w_hbm.at[:, pl.ds(HALF * p, HALF)], wbuf.at[p, 0, 0, 0])
    load(feat_hbm, featb)
    load(rate_hbm, rate_ref)
    load(taps_hbm, taps_ref)
    load(res_hbm, res_ref)
    load(skip_hbm, skip_ref)
    pl.semaphore_wait(barrier, len(partners))

    def here(round_of):
        if round_of:
            pl.semaphore_wait(here_sem.at[round_of - 1], len(around))
        if round_of < 3:
            for partner in around:
                pl.semaphore_signal(
                    here_sem.at[round_of], inc=1, device_id=partner, device_id_type=MESH
                )

    streams = [(p, d) for d in (0, 1) for p in (0, 1)]
    last = len(GROUPS) - 1

    def carried(d, k):
        return range(last + 1) if k < 3 else (range(3) if d == 0 else range(3, last + 1))

    ring1 = {st: copies.ids(4) for st in streams}
    ring2 = {
        (st, k, group): copies.ids(1)
        for st in streams for k in range(4) for group in carried(st[1], k)
    }
    over = [copies.ids(2) for _ in GROUPS]

    def slot(d, k):
        return 0 if k == 0 else N - 1 if k == N // 2 else 2 * k - d

    def target(p, d, inner):
        along_z = (p == 0) == inner
        return at(y, ring(z, DIRS[d]), c) if along_z else at(ring(y, DIRS[d]), z, c)

    def send1(p, d, k):
        src, dst = wbuf.at[p, 0, 0, slot(d, k)], wbuf.at[p, 0, 0, slot(d, k + 1)]
        copies.send(ring1[p, d] + k, src, dst, target(p, d, True))

    def recv1(p, d, k):
        ref = wbuf.at[p, 0, 0, slot(d, k + 1)]
        copies.make(ring1[p, d] + k, ref, ref, sib).wait_recv()

    def outer(p, d, k, group, core=0):
        low, high = GROUPS[group]
        return wbuf.at[p, core, slot(d, k), low:high]

    def send2(p, d, k, group):
        src, dst = outer(p, d, k, group), outer(p, d, k + 1, group)
        copies.send(ring2[(p, d), k, group], src, dst, target(p, d, False))

    def recv2(p, d, k, group):
        ref = outer(p, d, k + 1, group)
        copies.make(ring2[(p, d), k, group], ref, ref, sib).wait_recv()

    def over_refs(m, core):
        low, high = GROUPS[m]
        return wbuf.at[0, core, low:high], wbuf.at[1, core, :, low:high]

    def stage(n):
        if 1 <= n <= 4:
            for p, d in streams:
                if n < 4 or d == 1:
                    recv1(p, d, n - 1)
                if n < 3 or (n == 3 and d == 1):
                    send1(p, d, n)
        if n == 0:
            for p, d in streams:
                send1(p, d, 0)
        if n <= last:
            for p, d in streams:
                send2(p, d, 0, n)
        for k in range(4):
            group = n - 1 - k
            if not 0 <= group <= last:
                continue
            for p, d in streams:
                if group not in carried(d, k):
                    continue
                recv2(p, d, k, group)
                if k < 3 and group in carried(d, k + 1):
                    send2(p, d, k + 1, group)
        if n >= 4:
            for p in (0, 1):
                src, dst = over_refs(n - 4, 0)[p], over_refs(n - 4, 1)[p]
                copies.send(over[n - 4] + p, src, dst, sib)

    def gathered(m):
        for p in (0, 1):
            ref = over_refs(m, 1)[p]
            copies.make(over[m] + p, ref, ref, sib).wait_recv()

    halo_id = copies.ids(1)
    copies.send(halo_id, feat_hbm.at[:, pl.ds(TOK - 8, 8), :], halo, (after, t))
    here(0)
    for copy in loads[:2]:
        copy.wait()
    stage(0)

    for copy in loads[2:]:
        copy.wait()
    taps[...] = taps_ref[...].astype(F32)
    rate = rate_ref[...]
    for k, span in enumerate((1, 16, 32, 64, 128)):
        dec[k] = jnp.exp(-rate * float(span))
    for group in range(3):
        for lane in range(LANES):
            cut = slice(lane * 128, (lane + 1) * 128)
            x[group, lane, pl.ds(8, TOK), :] = featb[group, :, cut].astype(F32)
    stage(1)
    here(1)
    copies.make(halo_id, halo, halo, sib).wait_recv()
    for group in range(3):
        for lane in range(LANES):
            cut = slice(lane * 128, (lane + 1) * 128)
            edge = jnp.where(s > 0, halo[group, :, cut].astype(F32), 0.0)
            x[group, lane, pl.ds(0, 8), :] = edge

    def row(ref, *index):
        return jnp.broadcast_to(ref[index], (BLK, 128))

    def mix(lane, carry):
        col_at = pl.ds(pl.multiple_of(lane * 128, 128), 128)

        def mixed(group):
            w = [row(taps, group, pl.ds(k, 1), col_at) for k in range(3)]
            v = [x[group, lane, pl.ds(6 + i, BLK, stride=STEPS), :] for i in range(STEPS + 2)]
            return [w[0] * v[i + 2] + w[1] * v[i + 1] + w[2] * v[i] for i in range(STEPS)]

        one, two = mixed(1), mixed(2)
        for i in range(STEPS):
            u[i, :, col_at] = one[i] * two[i]
        for i, value in enumerate(mixed(0)):
            m0[i, :, col_at] = value
        return carry

    lax.fori_loop(0, LANES, mix, 0)

    block = lax.broadcasted_iota(jnp.int32, (BLK, 128), 0)

    def shifted(value, by):
        return jnp.where(block >= by, pltpu.roll(value, by, axis=0), 0.0)

    def pass1(lane, carry):
        col_at = pl.ds(pl.multiple_of(lane * 128, 128), 128)
        values = [u[i, :, col_at] for i in range(STEPS)]
        for pole in range(POLES):
            fade = row(dec, 0, pl.ds(pole, 1), col_at)
            state = values[0]
            for i in range(1, STEPS):
                state = fade * state + values[i]
            for k, by in ((1, 1), (2, 2), (3, 4)):
                state = state + row(dec, k, pl.ds(pole, 1), col_at) * shifted(state, by)
            ent[pole, :, col_at] = shifted(state, 1)
            ends[pl.ds(pole, 1), col_at] = state[BLK - 1 :, :]
        return carry

    lax.fori_loop(0, LANES, pass1, 0)
    ends_b[...] = ends[...].astype(BF16)
    sib_id = copies.ids(1)
    copies.send(sib_id, ends_b, sib_ends, sib)
    here(2)
    stage(2)

    mine = pl.ds(pl.multiple_of(c * HALF, HALF), HALF)
    rate_h = rate_ref[:, mine]

    def decay(tokens):
        return jnp.exp(-rate_h * float(tokens))

    copies.make(sib_id, sib_ends, sib_ends, sib).wait_recv()
    own_end, other_end = ends[:, mine], sib_ends[:, mine].astype(F32)
    first_end = jnp.where(c == 0, own_end, other_end)
    second_end = jnp.where(c == 0, other_end, own_end)
    total = decay(128) * first_end + second_end
    chip_end[...] = total.astype(BF16)

    here(3)
    y_id, z_id = copies.ids(N), copies.ids(N)
    y_held, z_held = copies.send_ids(N), copies.send_ids(N)
    for k in range(1, N):

        @pl.when(y + k < N)
        def _(k=k):
            copies.make(y_id + k, chip_end, y_in.at[k], at(y + k, z, c), y_held + k).start()

    stage(3)
    stage(4)

    col[...] = jnp.zeros_like(col)
    for k in range(1, N):

        @pl.when(y >= k)
        def _(k=k):
            copies.make(y_id + k, y_in.at[k], y_in.at[k], sib).wait_recv()
            col[...] += decay(2048 * (k - 1)) * y_in[k].astype(F32)

    col_b[...] = col[...].astype(BF16)
    colp_b[...] = (total + decay(2048) * col[...]).astype(BF16)
    for k in range(1, N):

        @pl.when(z + k < N)
        def _(k=k):
            copies.make(z_id + k, colp_b, z_in.at[k], at(y, z + k, c), z_held + k).start()

        @pl.when(z + k >= N)
        def _(k=k):
            copies.make(z_id + k, col_b, z_in.at[k], at(y, z + k - N, c), z_held + k).start()

    stage(5)
    stage(6)

    state = decay(256 * 7) * col[...]
    for k in range(1, N):
        copies.make(z_id + k, z_in.at[k], z_in.at[k], sib).wait_recv()
        state = state + decay(256 * (k - 1)) * z_in[k].astype(F32)
    enter_b[...] = state.astype(BF16)
    enter[:, mine] = state
    enter_id = copies.ids(1)
    copies.send(enter_id, enter_b, sib_enter, sib)
    copies.make(enter_id, sib_enter, sib_enter, sib).wait_recv()
    theirs = pl.ds(pl.multiple_of((1 - c) * HALF, HALF), HALF)
    enter[:, theirs] = sib_enter[...].astype(F32)

    @pl.when(c == 1)
    def _():
        enter[...] = dec[4] * enter[...] + sib_ends[...].astype(F32)


    far = (-float(STEPS)) * block.astype(F32)

    def pass2(lane, carry):
        col_at = pl.ds(pl.multiple_of(lane * 128, 128), 128)
        values = [u[i, :, col_at] for i in range(STEPS)]
        skip = row(skip_ref, pl.ds(0, 1), col_at)

        def one_pole(pole, sums):
            fade = row(dec, 0, pl.ds(pole, 1), col_at)
            gain = row(res_ref, pl.ds(pole, 1), col_at)
            reach = jnp.exp(far * row(rate_ref, pl.ds(pole, 1), col_at))
            state = ent[pole, :, col_at] + reach * row(enter, pl.ds(pole, 1), col_at)
            out = []
            for i in range(STEPS):
                state = fade * state + values[i]
                out.append(sums[i] + gain * state)
            return out

        sums = [skip * value for value in values]
        for pole in range(POLES):
            sums = one_pole(pole, sums)
        for i in range(STEPS):
            g[lane, pl.ds(i, BLK, stride=STEPS), :] = m0[i, :, col_at] * sums[i]
        return carry

    lax.fori_loop(0, LANES, pass2, 0)
    for lane in range(LANES):
        gb[:, lane * 128 : (lane + 1) * 128] = g[lane].astype(BF16)

    def near(of, home_at):
        off = lax.rem(of - home_at + N, N)
        return jnp.where(off <= N // 2, jnp.maximum(2 * off - 1, 0), 2 * (N - off))

    z_slots = [near(i, z) for i in range(N)]
    cores = [c, 1 - c]
    units = [off for offsets in OFFSETS for off in offsets]
    rs, rs_held = copies.ids(12), copies.send_ids(12)
    top, low = pl.ds(0, TOK // 2), pl.ds(TOK // 2, TOK // 2)
    next_dev, prev_dev = (s, x_next), (s, x_prev)

    def place(off):
        y_of = ring(y, off)
        return lax.rem(lax.div(y_of, 2) - t + 4, 4), lax.rem(y_of, 2)

    def project(y_slot, n):
        total = None
        for p in range(2):
            rows = []
            for i in range(8 * n, 8 * n + 8):
                at_z, core = z_slots[i // 2], cores[i % 2]
                rows.append(wbuf[0, core, y_slot, at_z] if p == 0 else wbuf[1, core, at_z, y_slot])
            term = lax.dot_general(
                gb[:, p * HALF : (p + 1) * HALF], jnp.concatenate(rows, axis=0),
                (((1,), (1,)), ((), ())), preferred_element_type=F32,
            )
            total = term if total is None else total + term
        return total

    def shipments(off):
        at_unit = units.index(off)
        _, odd = place(off)
        mine_top, mine_low = part.at[at_unit, top], part.at[at_unit, low]
        far_at, near_at = 2 * odd, 4 + 4 * odd
        far = [(far_at, mine_top, diag.at[at_unit], prev_dev), (far_at + 1, mine_low, diag.at[at_unit], next_dev)]
        nxt = [(near_at, mine_top, arrived.at[odd, 0, top], next_dev), (near_at + 1, mine_low, arrived.at[odd, 0, low], next_dev)]
        prv = [(near_at + 2, mine_low, arrived.at[odd, 1, low], prev_dev), (near_at + 3, mine_top, arrived.at[odd, 1, top], prev_dev)]
        return {
            role: [functools.partial(copies.make, rs + k, *rest, rs_held + k) for k, *rest in ships]
            for role, ships in ((2, far), (1, nxt), (3, prv))
        }

    def begin(off):
        at_unit = units.index(off)
        role, odd = place(off)
        y_slot = at_unit
        for n in range(2):
            cols = slice(n * 256, (n + 1) * 256)
            total = project(y_slot, n)
            part[at_unit, :, cols] = total.astype(BF16)

            @pl.when(role == 0)
            def _(total=total, cols=cols):
                own[odd, :, cols] = total

        ships = shipments(off)

        @pl.when(role == 2)
        def _():
            ships[2][0]().start()
            ships[2][1]().start()

        for side in (1, 3):

            @pl.when(role == side)
            def _(side=side):
                ships[side][0]().start()

    def relay(off):
        at_unit = units.index(off)
        role, odd = place(off)
        ships = shipments(off)
        for side, index, rows in ((1, 1, low), (3, 0, top)):

            @pl.when(role == side)
            def _(side=side, index=index, rows=rows):
                copies.make(rs + 2 * odd + index, diag.at[at_unit], diag.at[at_unit], sib).wait_recv()
                total = part[at_unit, rows, :].astype(F32) + diag[at_unit].astype(F32)
                part[at_unit, rows, :] = total.astype(BF16)
                ships[side][1]().start()

    def finish(off):
        role, odd = place(off)
        ships = shipments(off)

        @pl.when(role == 0)
        def _():
            for k, side, rows in ((0, 0, top), (1, 0, low), (2, 1, low), (3, 1, top)):
                ref = arrived.at[odd, side, rows]
                copies.make(rs + 4 + 4 * odd + k, ref, ref, sib).wait_recv()
            total = own[odd] + arrived[odd, 0].astype(F32) + arrived[odd, 1].astype(F32)
            out_ref[:, pl.ds(pl.multiple_of(odd * WIDE, WIDE), WIDE)] = total.astype(BF16)

        for side in (1, 2, 3):

            @pl.when(role == side)
            def _(side=side):
                for copy in ships[side]:
                    copy().wait_send()

    gathered(0)
    begin(0)
    gathered(1)
    begin(1)
    begin(-1)
    stage(7)
    gathered(2)
    begin(2)
    begin(-2)
    relay(0)
    relay(1)
    relay(-1)
    gathered(3)
    begin(3)
    begin(-3)
    stage(8)
    gathered(4)
    begin(4)
    relay(2)
    relay(-2)
    relay(3)
    relay(-3)
    relay(4)
    for off in units:
        finish(off)

    assert (copies.used, copies.held) == (N_RECV, N_SEND)
    for copy in copies.pool.values():
        copy.wait_send()
    for k in range(1, N):

        @pl.when(y + k < N)
        def _(k=k):
            copies.make(y_id + k, chip_end, y_in.at[k], sib, y_held + k).wait_send()

        copies.make(z_id + k, col_b, z_in.at[k], sib, z_held + k).wait_send()


N_RECV, N_SEND = 127, POOL + 28


def per_device(features, short_taps, rates, residues, skip, out_weight):
    vmem, hbm = pl.BlockSpec(memory_space=pltpu.VMEM), pl.BlockSpec(memory_space=pltpu.HBM)
    return pl.pallas_call(
        kernel,
        out_shape=jax.ShapeDtypeStruct((TOK, CH), BF16),
        in_specs=[hbm] * 6,
        out_specs=vmem,
        scratch_shapes=[
            pltpu.VMEM((2, 2, N, N, 32, HALF), BF16),
            pltpu.VMEM((3, TOK, CH), BF16),
            pltpu.VMEM((3, 8, CH), BF16),
            pltpu.VMEM((3, LANES, TOK + 8, 128), F32),
            pltpu.VMEM((STEPS, BLK, CH), F32),
            pltpu.VMEM((STEPS, BLK, CH), F32),
            pltpu.VMEM((3, 3, CH), BF16),
            pltpu.VMEM((POLES, CH), F32),
            pltpu.VMEM((POLES, CH), F32),
            pltpu.VMEM((1, CH), F32),
            pltpu.VMEM((3, 3, CH), F32),
            pltpu.VMEM((5, POLES, CH), F32),
            pltpu.VMEM((POLES, BLK, CH), F32),
            pltpu.VMEM((POLES, CH), F32),
            pltpu.VMEM((POLES, CH), BF16),
            pltpu.VMEM((POLES, CH), BF16),
            pltpu.VMEM((POLES, HALF), BF16),
            pltpu.VMEM((N, POLES, HALF), BF16),
            pltpu.VMEM((POLES, HALF), BF16),
            pltpu.VMEM((POLES, HALF), BF16),
            pltpu.VMEM((N, POLES, HALF), BF16),
            pltpu.VMEM((POLES, HALF), F32),
            pltpu.VMEM((POLES, CH), F32),
            pltpu.VMEM((POLES, HALF), BF16),
            pltpu.VMEM((POLES, HALF), BF16),
            pltpu.VMEM((LANES, TOK, 128), F32),
            pltpu.VMEM((TOK, CH), BF16),
            pltpu.VMEM((2, TOK, WIDE), F32),
            pltpu.VMEM((N, TOK, WIDE), BF16),
            pltpu.VMEM((N, TOK // 2, WIDE), BF16),
            pltpu.VMEM((2, 2, TOK, WIDE), BF16),
            pltpu.SemaphoreType.DMA((N_SEND,)),
            pltpu.SemaphoreType.DMA((N_RECV,)),
            pltpu.SemaphoreType.DMA((7,)),
            pltpu.SemaphoreType.REGULAR((3,)),
        ],
        compiler_params=pltpu.CompilerParams(
            collective_id=0, has_side_effects=True, vmem_limit_bytes=67043328
        ),
        name="hyena",
    )(
        features.transpose(1, 0, 2),
        short_taps,
        rates.T,
        residues.T,
        skip.reshape(1, CH),
        out_weight,
    )


def solution(mesh):
    in_specs = (
        P("seq", None, "tp"),
        P(None, None, "tp"),
        P("tp", None),
        P("tp", None),
        P("tp"),
        P("seq", "tp"),
    )
    out_specs = P("seq", "tp")
    return jax.shard_map(
        per_device, mesh=mesh, in_specs=in_specs, out_specs=out_specs, check_vma=False
    )
```

time: 73.5 us -> 66.8 us (0.909)
  the two profiles are of different devices: /device:TPU:1 before, /device:TPU:32 now
where the time goes in v2:
time: 66.8 us; the launch traced here: 66.7 us
  Pallas kernels  65 us (97%)
  local copies, waits for them, and re-layouts  1.67 us (2%)
    pallas_call x1, Pallas kernels, per_device(): pl.pallas_call(kernel, out_shape=jax.ShapeDtypeStruct((TOK, CH), BF16), i...  65 us
    unnamed x1, local copies, waits for them, and re-layouts  1.67 us

profile of v2, /device:TPU:32, one launch (start us, length us, event | category | flops | bytes accessed | tf_op | source)
XLA Modules:
  0.0 66.7 jit_solution(9640312677200867199)
XLA Ops:
  0.0 65.0 %hyena.1 = bf16[128,1024]{1,0:T(8,128)(2,1)} custom-call(bf16[3,128,1024]{2,1,0:T(8,128)(2,1)} %bitcast.4, bf16[3,3,1024]{2,1,0:T(4,128)(2,1)} %taps_hbm.1, f32[16,1024]{1,0:T(8,128)} %bitcast.5, f32[16,1024]{1,0:T(8,128)} %bitcast.6, f32[1,1024]{1,0:T(1,128)} %bitcast.7, bf16[32,1024]{1,0:T(8,128)(2,1)} %w_hbm.1), custom_call_target="tpu_custom_call" | custom-call | tf_op jit(solution)/shard_map/hyena/pallas_call | solution.py:496
  65.0 1.7 %copy.8 = bf16[128,1024]{1,0:T(8,128)(2,1)} copy(bf16[128,1024]{1,0:T(8,128)(2,1)} %hyena.1) | data formatting | bytes 524288

commit v3 on v2

--- a/solution.py
+++ b/solution.py
@@ -15,10 +15,11 @@
 LANES = CH // 128
 HALF = CH // 2
 DIRS = (1, -1)
-POOL = 64
+POOL = 32
 GROUPS = ((0, 1), (1, 3), (3, 5), (5, 7), (7, 8))
 OFFSETS = ((0,), (1, -1), (2, -2), (3, -3), (4,))
 WIDE = 512
+SPLIT = 6
 
 
 class Copies:
@@ -57,7 +58,7 @@
     feat_hbm, taps_hbm, rate_hbm, res_hbm, skip_hbm, w_hbm, out_ref,
     wbuf, featb, halo, x, u, m0, taps_ref, rate_ref, res_ref, skip_ref, taps, dec,
     ent, ends, ends_b, sib_ends, chip_end, y_in, col_b, colp_b, z_in, col, enter,
-    enter_b, sib_enter, g, gb, own, part, diag, arrived,
+    enter_b, sib_enter, g, gb, own, part, diag, arrived, done, pick,
     send_sem, recv_sem, local_sem, here_sem,
 ):
     s, t = lax.axis_index("seq"), lax.axis_index("tp")
@@ -118,7 +119,7 @@
         (st, k, group): copies.ids(1)
         for st in streams for k in range(4) for group in carried(st[1], k)
     }
-    over = [copies.ids(2) for _ in GROUPS]
+    over = [copies.ids(2) for _ in range(6)]
 
     def slot(d, k):
         return 0 if k == 0 else N - 1 if k == N // 2 else 2 * k - d
@@ -148,8 +149,9 @@
         copies.make(ring2[(p, d), k, group], ref, ref, sib).wait_recv()
 
     def over_refs(m, core):
-        low, high = GROUPS[m]
-        return wbuf.at[0, core, low:high], wbuf.at[1, core, :, low:high]
+        low, high = GROUPS[min(m, last)]
+        first, end = ((0, N), (0, SPLIT), (SPLIT, N))[max(m - last + 1, 0)]
+        return wbuf.at[0, core, low:high, first:end], wbuf.at[1, core, first:end, low:high]
 
     def stage(n):
         if 1 <= n <= 4:
@@ -174,10 +176,9 @@
                 recv2(p, d, k, group)
                 if k < 3 and group in carried(d, k + 1):
                     send2(p, d, k + 1, group)
-        if n >= 4:
+        for m in {4: (0,), 5: (1,), 6: (2,), 7: (3, 4), 8: (5,)}.get(n, ()):
             for p in (0, 1):
-                src, dst = over_refs(n - 4, 0)[p], over_refs(n - 4, 1)[p]
-                copies.send(over[n - 4] + p, src, dst, sib)
+                copies.send(over[m] + p, over_refs(m, 0)[p], over_refs(m, 1)[p], sib)
 
     def gathered(m):
         for p in (0, 1):
@@ -256,6 +257,17 @@
     here(2)
     stage(2)
 
+    def choose(n, carry):
+        rows = pl.ds(pl.multiple_of(n * 128, 128), 128)
+        from_at = lax.broadcasted_iota(jnp.int32, (128, WIDE), 0) + n * 128
+        to_at = lax.broadcasted_iota(jnp.int32, (128, WIDE), 1)
+        off = ((to_at >> 6) - z + N) & (N - 1)
+        at_slot = jnp.where(off <= N // 2, jnp.maximum(2 * off - 1, 0), 2 * (N - off))
+        pick[rows, :] = (from_at == at_slot * 64 + (to_at & 63)).astype(F32).astype(BF16)
+        return carry
+
+    lax.fori_loop(0, WIDE // 128, choose, 0)
+
     mine = pl.ds(pl.multiple_of(c * HALF, HALF), HALF)
     rate_h = rate_ref[:, mine]
 
@@ -302,7 +314,6 @@
             copies.make(z_id + k, col_b, z_in.at[k], at(y, z + k - N, c), z_held + k).start()
 
     stage(5)
-    stage(6)
 
     state = decay(256 * 7) * col[...]
     for k in range(1, N):
@@ -312,6 +323,7 @@
     enter[:, mine] = state
     enter_id = copies.ids(1)
     copies.send(enter_id, enter_b, sib_enter, sib)
+    stage(6)
     copies.make(enter_id, sib_enter, sib_enter, sib).wait_recv()
     theirs = pl.ds(pl.multiple_of((1 - c) * HALF, HALF), HALF)
     enter[:, theirs] = sib_enter[...].astype(F32)
@@ -350,14 +362,10 @@
     for lane in range(LANES):
         gb[:, lane * 128 : (lane + 1) * 128] = g[lane].astype(BF16)
 
-    def near(of, home_at):
-        off = lax.rem(of - home_at + N, N)
-        return jnp.where(off <= N // 2, jnp.maximum(2 * off - 1, 0), 2 * (N - off))
-
-    z_slots = [near(i, z) for i in range(N)]
     cores = [c, 1 - c]
-    units = [off for offsets in OFFSETS for off in offsets]
-    rs, rs_held = copies.ids(12), copies.send_ids(12)
+    units = [(off, 0, N) for offsets in OFFSETS[:4] for off in offsets]
+    units += [(4, 0, SPLIT), (4, SPLIT, N)]
+    rs = {later: (copies.ids(12), copies.send_ids(12)) for later in (False, True)}
     top, low = pl.ds(0, TOK // 2), pl.ds(TOK // 2, TOK // 2)
     next_dev, prev_dev = (s, x_next), (s, x_prev)
 
@@ -365,13 +373,13 @@
         y_of = ring(y, off)
         return lax.rem(lax.div(y_of, 2) - t + 4, 4), lax.rem(y_of, 2)
 
-    def project(y_slot, n):
+    def project(y_slot, first, end):
         total = None
         for p in range(2):
             rows = []
-            for i in range(8 * n, 8 * n + 8):
-                at_z, core = z_slots[i // 2], cores[i % 2]
-                rows.append(wbuf[0, core, y_slot, at_z] if p == 0 else wbuf[1, core, at_z, y_slot])
+            for at_z in range(first, end):
+                for core in cores:
+                    rows.append(wbuf[0, core, y_slot, at_z] if p == 0 else wbuf[1, core, at_z, y_slot])
             term = lax.dot_general(
                 gb[:, p * HALF : (p + 1) * HALF], jnp.concatenate(rows, axis=0),
                 (((1,), (1,)), ((), ())), preferred_element_type=F32,
@@ -379,33 +387,35 @@
             total = term if total is None else total + term
         return total
 
-    def shipments(off):
-        at_unit = units.index(off)
+    def shipments(unit):
+        at_unit, (off, first, end) = min(unit, N - 1), units[unit]
         _, odd = place(off)
-        mine_top, mine_low = part.at[at_unit, top], part.at[at_unit, low]
+        ids, held = rs[first > 0]
+        cols = pl.ds(64 * first, 64 * (end - first))
+        mine_top, mine_low = part.at[at_unit, top, cols], part.at[at_unit, low, cols]
         far_at, near_at = 2 * odd, 4 + 4 * odd
-        far = [(far_at, mine_top, diag.at[at_unit], prev_dev), (far_at + 1, mine_low, diag.at[at_unit], next_dev)]
-        nxt = [(near_at, mine_top, arrived.at[odd, 0, top], next_dev), (near_at + 1, mine_low, arrived.at[odd, 0, low], next_dev)]
-        prv = [(near_at + 2, mine_low, arrived.at[odd, 1, low], prev_dev), (near_at + 3, mine_top, arrived.at[odd, 1, top], prev_dev)]
+        far = [(far_at, mine_top, diag.at[at_unit, :, cols], prev_dev), (far_at + 1, mine_low, diag.at[at_unit, :, cols], next_dev)]
+        nxt = [(near_at, mine_top, arrived.at[odd, 0, top, cols], next_dev), (near_at + 1, mine_low, arrived.at[odd, 0, low, cols], next_dev)]
+        prv = [(near_at + 2, mine_low, arrived.at[odd, 1, low, cols], prev_dev), (near_at + 3, mine_top, arrived.at[odd, 1, top, cols], prev_dev)]
         return {
-            role: [functools.partial(copies.make, rs + k, *rest, rs_held + k) for k, *rest in ships]
+            role: [functools.partial(copies.make, ids + k, *rest, held + k) for k, *rest in ships]
             for role, ships in ((2, far), (1, nxt), (3, prv))
         }
 
-    def begin(off):
-        at_unit = units.index(off)
+    def begin(at):
+        at_unit, (off, first, end) = min(at, N - 1), units[at]
         role, odd = place(off)
-        y_slot = at_unit
-        for n in range(2):
-            cols = slice(n * 256, (n + 1) * 256)
-            total = project(y_slot, n)
+        for start in range(first, end, 4):
+            stop = min(start + 4, end)
+            cols = slice(start * 64, stop * 64)
+            total = project(at_unit, start, stop)
             part[at_unit, :, cols] = total.astype(BF16)
 
             @pl.when(role == 0)
             def _(total=total, cols=cols):
                 own[odd, :, cols] = total
 
-        ships = shipments(off)
+        ships = shipments(at)
 
         @pl.when(role == 2)
         def _():
@@ -418,30 +428,35 @@
             def _(side=side):
                 ships[side][0]().start()
 
-    def relay(off):
-        at_unit = units.index(off)
+    def relay(at):
+        at_unit, (off, first, end) = min(at, N - 1), units[at]
         role, odd = place(off)
-        ships = shipments(off)
+        ships = shipments(at)
+        cols = slice(64 * first, 64 * end)
         for side, index, rows in ((1, 1, low), (3, 0, top)):
 
             @pl.when(role == side)
             def _(side=side, index=index, rows=rows):
-                copies.make(rs + 2 * odd + index, diag.at[at_unit], diag.at[at_unit], sib).wait_recv()
-                total = part[at_unit, rows, :].astype(F32) + diag[at_unit].astype(F32)
-                part[at_unit, rows, :] = total.astype(BF16)
+                ref = diag.at[at_unit, :, cols]
+                copies.make(rs[first > 0][0] + 2 * odd + index, ref, ref, sib).wait_recv()
+                total = part[at_unit, rows, cols].astype(F32) + ref[...].astype(F32)
+                part[at_unit, rows, cols] = total.astype(BF16)
                 ships[side][1]().start()
 
-    def finish(off):
+    def finish(at):
+        off, first, end = units[at]
         role, odd = place(off)
-        ships = shipments(off)
+        ships = shipments(at)
+        cols = slice(64 * first, 64 * end)
 
         @pl.when(role == 0)
         def _():
             for k, side, rows in ((0, 0, top), (1, 0, low), (2, 1, low), (3, 1, top)):
-                ref = arrived.at[odd, side, rows]
-                copies.make(rs + 4 + 4 * odd + k, ref, ref, sib).wait_recv()
-            total = own[odd] + arrived[odd, 0].astype(F32) + arrived[odd, 1].astype(F32)
-            out_ref[:, pl.ds(pl.multiple_of(odd * WIDE, WIDE), WIDE)] = total.astype(BF16)
+                ref = arrived.at[odd, side, rows, cols]
+                copies.make(rs[first > 0][0] + 4 + 4 * odd + k, ref, ref, sib).wait_recv()
+            total = own[odd, :, cols] + arrived[odd, 0, :, cols].astype(F32)
+            total = total + arrived[odd, 1, :, cols].astype(F32)
+            done[odd, :, cols] = total.astype(BF16)
 
         for side in (1, 2, 3):
 
@@ -454,27 +469,35 @@
     begin(0)
     gathered(1)
     begin(1)
-    begin(-1)
+    begin(2)
     stage(7)
     gathered(2)
-    begin(2)
-    begin(-2)
+    begin(3)
+    begin(4)
+    gathered(3)
+    begin(5)
+    begin(6)
+    gathered(4)
+    begin(7)
+    stage(8)
     relay(0)
     relay(1)
-    relay(-1)
-    gathered(3)
-    begin(3)
-    begin(-3)
-    stage(8)
-    gathered(4)
-    begin(4)
     relay(2)
-    relay(-2)
+    gathered(5)
+    begin(8)
     relay(3)
-    relay(-3)
     relay(4)
-    for off in units:
-        finish(off)
+    relay(5)
+    relay(6)
+    relay(7)
+    relay(8)
+    for at in range(len(units)):
+        finish(at)
+    for odd in (0, 1):
+        cols = lax.dot_general(
+            done[odd], pick[...], (((1,), (0,)), ((), ())), preferred_element_type=F32
+        )
+        out_ref[:, odd * WIDE : (odd + 1) * WIDE] = cols.astype(BF16)
 
     assert (copies.used, copies.held) == (N_RECV, N_SEND)
     for copy in copies.pool.values():
@@ -488,7 +511,7 @@
         copies.make(z_id + k, col_b, z_in.at[k], sib, z_held + k).wait_send()
 
 
-N_RECV, N_SEND = 127, POOL + 28
+N_RECV, N_SEND = 141, POOL + 40
 
 
 def per_device(features, short_taps, rates, residues, skip, out_weight):
@@ -530,6 +553,8 @@
             pltpu.VMEM((N, TOK, WIDE), BF16),
             pltpu.VMEM((N, TOK // 2, WIDE), BF16),
             pltpu.VMEM((2, 2, TOK, WIDE), BF16),
+            pltpu.VMEM((2, TOK, WIDE), BF16),
+            pltpu.VMEM((WIDE, WIDE), BF16),
             pltpu.SemaphoreType.DMA((N_SEND,)),
             pltpu.SemaphoreType.DMA((N_RECV,)),
             pltpu.SemaphoreType.DMA((7,)),

time: 66.8 us -> 63 us (0.943)
  the two profiles are of different devices: /device:TPU:32 before, /device:TPU:1 now
where the time goes in v3:
time: 63 us; the launch traced here: 62.2 us
  Pallas kernels  60.5 us (96%)
  local copies, waits for them, and re-layouts  1.67 us (3%)
    pallas_call x1, Pallas kernels, per_device(): pl.pallas_call(kernel, out_shape=jax.ShapeDtypeStruct((TOK, CH), BF16), i...  60.5 us
    unnamed x1, local copies, waits for them, and re-layouts  1.67 us

profile of v3, /device:TPU:1, one launch (start us, length us, event | category | flops | bytes accessed | tf_op | source)
XLA Modules:
  0.0 62.2 jit_solution(3007217034294701402)
XLA Ops:
  0.0 60.5 %hyena.1 = bf16[128,1024]{1,0:T(8,128)(2,1)} custom-call(bf16[3,128,1024]{2,1,0:T(8,128)(2,1)} %bitcast.4, bf16[3,3,1024]{2,1,0:T(4,128)(2,1)} %taps_hbm.1, f32[16,1024]{1,0:T(8,128)} %bitcast.5, f32[16,1024]{1,0:T(8,128)} %bitcast.6, f32[1,1024]{1,0:T(1,128)} %bitcast.7, bf16[32,1024]{1,0:T(8,128)(2,1)} %w_hbm.1), custom_call_target="tpu_custom_call" | custom-call | tf_op jit(solution)/shard_map/hyena/pallas_call | solution.py:519
  60.5 1.7 %copy.8 = bf16[128,1024]{1,0:T(8,128)(2,1)} copy(bf16[128,1024]{1,0:T(8,128)(2,1)} %hyena.1) | data formatting | bytes 524288

commit v4 on v3

--- a/solution.py
+++ b/solution.py
@@ -15,7 +15,7 @@
 LANES = CH // 128
 HALF = CH // 2
 DIRS = (1, -1)
-POOL = 32
+POOL = 24
 GROUPS = ((0, 1), (1, 3), (3, 5), (5, 7), (7, 8))
 OFFSETS = ((0,), (1, -1), (2, -2), (3, -3), (4,))
 WIDE = 512
@@ -360,7 +360,7 @@
 
     lax.fori_loop(0, LANES, pass2, 0)
     for lane in range(LANES):
-        gb[:, lane * 128 : (lane + 1) * 128] = g[lane].astype(BF16)
+        gb[:, lane * 128 : (lane + 1) * 128] = g[lane, pl.ds(0, TOK), :].astype(BF16)
 
     cores = [c, 1 - c]
     units = [(off, 0, N) for offsets in OFFSETS[:4] for off in offsets]
@@ -480,19 +480,26 @@
     gathered(4)
     begin(7)
     stage(8)
+    gathered(5)
+    begin(8)
     relay(0)
     relay(1)
     relay(2)
-    gathered(5)
-    begin(8)
     relay(3)
     relay(4)
     relay(5)
     relay(6)
     relay(7)
     relay(8)
-    for at in range(len(units)):
-        finish(at)
+    finish(0)
+    finish(1)
+    finish(2)
+    finish(3)
+    finish(4)
+    finish(5)
+    finish(6)
+    finish(7)
+    finish(8)
     for odd in (0, 1):
         cols = lax.dot_general(
             done[odd], pick[...], (((1,), (0,)), ((), ())), preferred_element_type=F32
@@ -525,7 +532,7 @@
             pltpu.VMEM((2, 2, N, N, 32, HALF), BF16),
             pltpu.VMEM((3, TOK, CH), BF16),
             pltpu.VMEM((3, 8, CH), BF16),
-            pltpu.VMEM((3, LANES, TOK + 8, 128), F32),
+            pltpu.VMEM((3, LANES, TOK + 24, 128), F32),
             pltpu.VMEM((STEPS, BLK, CH), F32),
             pltpu.VMEM((STEPS, BLK, CH), F32),
             pltpu.VMEM((3, 3, CH), BF16),
@@ -547,7 +554,7 @@
             pltpu.VMEM((POLES, CH), F32),
             pltpu.VMEM((POLES, HALF), BF16),
             pltpu.VMEM((POLES, HALF), BF16),
-            pltpu.VMEM((LANES, TOK, 128), F32),
+            pltpu.VMEM((LANES, TOK + STEPS, 128), F32),
             pltpu.VMEM((TOK, CH), BF16),
             pltpu.VMEM((2, TOK, WIDE), F32),
             pltpu.VMEM((N, TOK, WIDE), BF16),

time: 63 us -> 62.8 us (level)
  no operation moved by 1% of the time
where the time goes in v4:
time: 62.8 us; the launch traced here: 62.1 us
  Pallas kernels  60.5 us (96%)
  local copies, waits for them, and re-layouts  1.67 us (3%)
    pallas_call x1, Pallas kernels, per_device(): pl.pallas_call(kernel, out_shape=jax.ShapeDtypeStruct((TOK, CH), BF16), i...  60.5 us
    unnamed x1, local copies, waits for them, and re-layouts  1.67 us

profile of v4, /device:TPU:1, one launch (start us, length us, event | category | flops | bytes accessed | tf_op | source)
XLA Modules:
  0.0 62.1 jit_solution(8462025995336705108)
XLA Ops:
  0.0 60.5 %hyena.1 = bf16[128,1024]{1,0:T(8,128)(2,1)} custom-call(bf16[3,128,1024]{2,1,0:T(8,128)(2,1)} %bitcast.4, bf16[3,3,1024]{2,1,0:T(4,128)(2,1)} %taps_hbm.1, f32[16,1024]{1,0:T(8,128)} %bitcast.5, f32[16,1024]{1,0:T(8,128)} %bitcast.6, f32[1,1024]{1,0:T(1,128)} %bitcast.7, bf16[32,1024]{1,0:T(8,128)(2,1)} %w_hbm.1), custom_call_target="tpu_custom_call" | custom-call | tf_op jit(solution)/shard_map/hyena/pallas_call | solution.py:526
  60.5 1.7 %copy.8 = bf16[128,1024]{1,0:T(8,128)(2,1)} copy(bf16[128,1024]{1,0:T(8,128)(2,1)} %hyena.1) | data formatting | bytes 524288
